TPU v7x, 32 devices: a whole 2x2x4 slice. The times are simulated.
32 devices in a mesh: fsdp: 8 (over y, x, core), seq: 4 (over z).
Axes of the slice: x: 2, y: 2, z: 4, core: 2. Of those that a mesh axis runs over, the one named last changes fastest.
Arguments:
- hidden_in: bfloat16 [8, 1024, 2048], P('fsdp', 'seq'), may hold values from -6 to 6
- lengths: int32 [8], P('fsdp'), may hold values from 512 to 1024, as said below
- cotangent: bfloat16 [8, 1024, 2048], P('fsdp', 'seq'), may hold values from -6 to 6
- in_weight: bfloat16 [2048, 6144], P(('fsdp', 'seq')), may hold values from -0.125 to 0.125
- in_bias: bfloat16 [6144], P(('fsdp', 'seq')), may hold values from -0.29882812 to 0.29882812
- out_weight: bfloat16 [2048, 2048], P(('fsdp', 'seq')), may hold values from -1 to 1
- out_bias: bfloat16 [2048], P(('fsdp', 'seq')), may hold values from -2 to 2
- up_weight: bfloat16 [8192, 2048], P(('fsdp', 'seq')), may hold values from -0.125 to 0.125
- up_bias: bfloat16 [8192], P(('fsdp', 'seq')), may hold values from -2 to 2
- down_weight: bfloat16 [8192, 2048], P(('fsdp', 'seq')), may hold values from -0.0625 to 0.0625
- down_bias: bfloat16 [2048], P(('fsdp', 'seq')), may hold values from -2 to 2
- first_gain: bfloat16 [2048], P(('fsdp', 'seq')), may hold values from 0.5 to 1.5
- first_shift: bfloat16 [2048], P(('fsdp', 'seq')), may hold values from -2 to 2
- second_gain: bfloat16 [2048], P(('fsdp', 'seq')), may hold values from 0.5 to 1.5
- second_shift: bfloat16 [2048], P(('fsdp', 'seq')), may hold values from -2 to 2
Outputs:
- layer_output: float32 [8, 1024, 2048], P('fsdp', 'seq')
- input_gradient: float32 [8, 1024, 2048], P('fsdp', 'seq')
- in_weight_gradient: float32 [2048, 6144], P(('fsdp', 'seq'))
- in_bias_gradient: float32 [6144], P(('fsdp', 'seq'))
- out_weight_gradient: float32 [2048, 2048], P(('fsdp', 'seq'))
- out_bias_gradient: float32 [2048], P(('fsdp', 'seq'))
- up_weight_gradient: float32 [8192, 2048], P(('fsdp', 'seq'))
- up_bias_gradient: float32 [8192], P(('fsdp', 'seq'))
- down_weight_gradient: float32 [8192, 2048], P(('fsdp', 'seq'))
- down_bias_gradient: float32 [2048], P(('fsdp', 'seq'))
- first_gain_gradient: float32 [2048], P(('fsdp', 'seq'))
- first_shift_gradient: float32 [2048], P(('fsdp', 'seq'))
- second_gain_gradient: float32 [2048], P(('fsdp', 'seq'))
- second_shift_gradient: float32 [2048], P(('fsdp', 'seq'))
Inputs may be any that keep to these rules, and one draw needn't show every extreme that they name: `lengths`: tokens in use at the front of each slot; in every draw one slot is full and one holds 512 tokens.
All inputs are finite; a program needn't handle non-finite values.
Results may differ from a plain program's by a relative error of at most 0.014.
Values may be sent and summed in bfloat16 or wider, within the bound.
No kernel may reach another device: no remote copies, remote signals or barrier semaphores. Data moves between devices by JAX's collectives and lax.ppermute only.
A program may use at most 384 MiB of HBM per device.

v0:
```python
import jax
import jax.numpy as jnp
from jax import lax
from jax.sharding import PartitionSpec as P

HEADS = 16
HEAD_DIM = 128
ROT = 32
EPSILON = 1e-05
MASKED_SCORE = -1e30


def layer_norm(values, norm_gain, norm_shift):
    centred = values - jnp.mean(values, axis=-1, keepdims=True)
    spread = jnp.mean(centred * centred, axis=-1, keepdims=True)
    return centred * lax.rsqrt(spread + EPSILON) * norm_gain + norm_shift


def rotary_tables(positions):
    halves = jnp.arange(ROT // 2, dtype=jnp.float32)
    frequency = 1.0 / 10000.0 ** (halves * 2.0 / ROT)
    angles = positions.astype(jnp.float32)[:, None] * frequency[None, :]
    angles = jnp.concatenate([angles, angles], axis=1)
    return (jnp.cos(angles), jnp.sin(angles))


def rotate(values, cosine_table, sine_table):
    leading = values[..., :ROT]
    middle = ROT // 2
    turned = jnp.concatenate([-leading[..., middle:], leading[..., :middle]], axis=-1)
    leading = leading * cosine_table[:, None, :] + turned * sine_table[:, None, :]
    return jnp.concatenate([leading, values[..., ROT:]], axis=-1)


def exact_gelu(values):
    return jax.nn.gelu(values, approximate=False)


def matmul(left_side, right_side):
    return jnp.dot(left_side, right_side, preferred_element_type=jnp.float32)


def times_transposed(left_side, right_side):
    return lax.dot_general(
        left_side, right_side, (((1,), (1,)), ((), ())), preferred_element_type=jnp.float32
    )


def transposed_times(left_side, right_side):
    return lax.dot_general(
        left_side, right_side, (((0,), (0,)), ((), ())), preferred_element_type=jnp.float32
    )


def attend_slot(query, key_rows, value_rows, keep_mask):
    length_full = query.shape[0]
    block_rows = min(512, length_full)
    block_count = length_full // block_rows
    columns = jnp.arange(length_full, dtype=jnp.int32)
    scale_factor = HEAD_DIM ** (-0.5)

    def one_block(first_row):
        row_index = first_row + jnp.arange(block_rows, dtype=jnp.int32)
        query_block = lax.dynamic_slice_in_dim(query, first_row, block_rows, 0)
        scores = (
            jnp.einsum("qhd,khd->hqk", query_block, key_rows, preferred_element_type=jnp.float32)
            * scale_factor
        )
        allowed = (columns[None, :] <= row_index[:, None]) & keep_mask[None, :]
        scores = jnp.where(allowed[None], scores, MASKED_SCORE)
        largest = jnp.max(scores, axis=-1, keepdims=True)
        weights = jnp.exp(scores - largest)
        totals = jnp.sum(weights, axis=-1, keepdims=True)
        probabilities = (weights / totals).astype(jnp.bfloat16)
        mixed = jnp.einsum(
            "hqk,khd->qhd", probabilities, value_rows, preferred_element_type=jnp.float32
        )
        return (mixed, (largest + jnp.log(totals))[..., 0])

    starts = jnp.arange(block_count, dtype=jnp.int32) * block_rows
    mixed, log_sums = lax.map(one_block, starts)
    return (mixed.reshape(length_full, query.shape[1], query.shape[2]), log_sums)


def attend_slot_back(query, key_rows, value_rows, keep_mask, log_sums, mixed_delta):
    length_full = query.shape[0]
    block_rows = min(512, length_full)
    block_count = length_full // block_rows
    columns = jnp.arange(length_full, dtype=jnp.int32)
    scale_factor = HEAD_DIM ** (-0.5)

    def one_block(carried, member):
        key_delta, value_delta = carried
        first_row, log_block = member
        row_index = first_row + jnp.arange(block_rows, dtype=jnp.int32)
        query_block = lax.dynamic_slice_in_dim(query, first_row, block_rows, 0)
        delta_block = lax.dynamic_slice_in_dim(mixed_delta, first_row, block_rows, 0)
        scores = (
            jnp.einsum("qhd,khd->hqk", query_block, key_rows, preferred_element_type=jnp.float32)
            * scale_factor
        )
        allowed = (columns[None, :] <= row_index[:, None]) & keep_mask[None, :]
        scores = jnp.where(allowed[None], scores, MASKED_SCORE)
        probabilities = jnp.where(allowed[None], jnp.exp(scores - log_block[..., None]), 0.0)
        prob_delta = jnp.einsum(
            "qhd,khd->hqk", delta_block, value_rows, preferred_element_type=jnp.float32
        )
        row_dot = jnp.sum(probabilities * prob_delta, axis=-1, keepdims=True)
        score_delta = (probabilities * (prob_delta - row_dot)).astype(jnp.bfloat16)
        query_delta = (
            jnp.einsum("hqk,khd->qhd", score_delta, key_rows, preferred_element_type=jnp.float32)
            * scale_factor
        )
        key_delta = (
            key_delta
            + jnp.einsum(
                "hqk,qhd->khd", score_delta, query_block, preferred_element_type=jnp.float32
            )
            * scale_factor
        )
        value_delta = value_delta + jnp.einsum(
            "hqk,qhd->khd",
            probabilities.astype(jnp.bfloat16),
            delta_block,
            preferred_element_type=jnp.float32,
        )
        return ((key_delta, value_delta), query_delta)

    starts = jnp.arange(block_count, dtype=jnp.int32) * block_rows
    zeroes = jnp.zeros(query.shape, jnp.float32)
    (key_delta, value_delta), query_delta = lax.scan(
        one_block, (zeroes, zeroes), (starts, log_sums)
    )
    return (query_delta.reshape(query.shape), key_delta, value_delta)


def feed_forward(inner_in, up_matrix, up_offset, down_matrix):
    hidden_pre = times_transposed(inner_in, up_matrix) + up_offset.astype(jnp.float32)
    hidden_act, pull_act = jax.vjp(exact_gelu, hidden_pre)
    hidden_low = hidden_act.astype(jnp.bfloat16)
    return (hidden_low, pull_act, matmul(hidden_low, down_matrix))


def feed_back(inner_in, hidden_low, pull_act, delta_rows, up_matrix, down_matrix):
    delta_down = transposed_times(hidden_low, delta_rows)
    delta_pre = pull_act(times_transposed(delta_rows, down_matrix))[0].astype(jnp.bfloat16)
    delta_up = transposed_times(delta_pre, inner_in)
    delta_up_bias = jnp.sum(delta_pre.astype(jnp.float32), axis=0)
    delta_inner = matmul(delta_pre, up_matrix)
    return (delta_up, delta_up_bias, delta_down, delta_inner)


def local(
    hidden_in,
    lengths,
    cotangent,
    in_weight,
    in_bias,
    out_weight,
    out_bias,
    up_weight,
    up_bias,
    down_weight,
    down_bias,
    first_gain,
    first_shift,
    second_gain,
    second_shift,
):
    slot_count, token_count, width = hidden_in.shape
    seq_count = lax.axis_size("seq")
    seq_index = lax.axis_index("seq")
    length_full = token_count * seq_count
    row_count = slot_count * token_count
    (
        in_matrix,
        in_offset,
        out_matrix,
        out_offset,
        gain_one,
        shift_one,
        gain_two,
        shift_two,
        down_offset,
    ) = (
        lax.all_gather(in_weight, ("fsdp", "seq"), axis=0, tiled=True),
        lax.all_gather(in_bias, ("fsdp", "seq"), axis=0, tiled=True),
        lax.all_gather(out_weight, ("fsdp", "seq"), axis=0, tiled=True),
        lax.all_gather(out_bias, ("fsdp", "seq"), axis=0, tiled=True),
        lax.all_gather(first_gain, ("fsdp", "seq"), axis=0, tiled=True),
        lax.all_gather(first_shift, ("fsdp", "seq"), axis=0, tiled=True),
        lax.all_gather(second_gain, ("fsdp", "seq"), axis=0, tiled=True),
        lax.all_gather(second_shift, ("fsdp", "seq"), axis=0, tiled=True),
        lax.all_gather(down_bias, ("fsdp", "seq"), axis=0, tiled=True),
    )
    positions = seq_index * token_count + jnp.arange(token_count, dtype=jnp.int32)
    keep_local = positions[None, :] < lengths[:, None]
    keep_full = jnp.arange(length_full, dtype=jnp.int32)[None, :] < lengths[:, None]
    source = hidden_in.astype(jnp.float32)
    normed_one, pull_one = jax.vjp(
        layer_norm, source, gain_one.astype(jnp.float32), shift_one.astype(jnp.float32)
    )
    first_in = normed_one.astype(jnp.bfloat16).reshape(row_count, width)
    cosine_table, sine_table = rotary_tables(positions)
    joined = matmul(first_in, in_matrix) + in_offset.astype(jnp.float32)
    joined = joined.reshape(slot_count, token_count, 3, HEADS, HEAD_DIM)

    def rotate_both(query_part, key_part):
        return (
            rotate(query_part, cosine_table, sine_table),
            rotate(key_part, cosine_table, sine_table),
        )

    turned, pull_turn = jax.vjp(rotate_both, joined[:, :, 0], joined[:, :, 1])
    query, key_rows, value_rows = (
        lax.all_to_all(
            turned[0].astype(jnp.bfloat16), "seq", split_axis=2, concat_axis=1, tiled=True
        ),
        lax.all_to_all(
            turned[1].astype(jnp.bfloat16), "seq", split_axis=2, concat_axis=1, tiled=True
        ),
        lax.all_to_all(
            joined[:, :, 2].astype(jnp.bfloat16), "seq", split_axis=2, concat_axis=1, tiled=True
        ),
    )
    mixed_heads, log_sums = jax.vmap(attend_slot)(query, key_rows, value_rows, keep_full)
    mixed = lax.all_to_all(
        mixed_heads.astype(jnp.bfloat16), "seq", split_axis=1, concat_axis=2, tiled=True
    ).reshape(row_count, width)
    attn_branch = matmul(mixed, out_matrix) + out_offset.astype(jnp.float32)
    normed_two, pull_two = jax.vjp(
        layer_norm, source, gain_two.astype(jnp.float32), shift_two.astype(jnp.float32)
    )
    second_in = normed_two.astype(jnp.bfloat16)
    delta_out = jnp.where(keep_local[..., None], cotangent.astype(jnp.float32), 0.0)
    delta_low = delta_out.astype(jnp.bfloat16)
    delta_rows = delta_low.reshape(row_count, width)
    up_matrix, up_offset, down_matrix = (
        lax.all_gather(up_weight, "fsdp", axis=0, tiled=True),
        lax.all_gather(up_bias, "fsdp", axis=0, tiled=True),
        lax.all_gather(down_weight, "fsdp", axis=0, tiled=True),
    )
    inner_in = lax.all_gather(second_in, "seq", axis=1, tiled=True).reshape(
        slot_count * length_full, width
    )
    hidden_low, pull_act, branch_part = feed_forward(inner_in, up_matrix, up_offset, down_matrix)
    branch_sum = lax.psum_scatter(
        branch_part.reshape(slot_count, length_full, width).astype(jnp.bfloat16),
        "seq",
        scatter_dimension=1,
        tiled=True,
    ).astype(jnp.float32)
    mlp_branch = branch_sum + down_offset.astype(jnp.float32)
    delta_all = lax.all_gather(delta_low, "seq", axis=1, tiled=True).reshape(
        slot_count * length_full, width
    )
    delta_up, delta_up_bias, delta_down, delta_inner = feed_back(
        inner_in, hidden_low, pull_act, delta_all, up_matrix, down_matrix
    )
    second_delta = lax.psum_scatter(
        delta_inner.reshape(slot_count, length_full, width).astype(jnp.bfloat16),
        "seq",
        scatter_dimension=1,
        tiled=True,
    ).astype(jnp.float32)
    up_gradient, up_bias_gradient, down_gradient = (
        lax.psum_scatter(
            delta_up.astype(jnp.bfloat16), "fsdp", scatter_dimension=0, tiled=True
        ).astype(jnp.float32),
        lax.psum_scatter(
            delta_up_bias.astype(jnp.bfloat16), "fsdp", scatter_dimension=0, tiled=True
        ).astype(jnp.float32),
        lax.psum_scatter(
            delta_down.astype(jnp.bfloat16), "fsdp", scatter_dimension=0, tiled=True
        ).astype(jnp.float32),
    )
    layer_output = jnp.where(
        keep_local[..., None],
        source + attn_branch.reshape(slot_count, token_count, width) + mlp_branch,
        0.0,
    )
    source_two, gain_two_delta, shift_two_delta = pull_two(second_delta)
    bias_sum = jnp.sum(delta_out.reshape(row_count, width), axis=0)
    out_delta = transposed_times(mixed, delta_rows)
    mixed_delta = times_transposed(delta_rows, out_matrix).astype(jnp.bfloat16)
    mixed_delta = lax.all_to_all(
        mixed_delta.reshape(slot_count, token_count, HEADS, HEAD_DIM),
        "seq",
        split_axis=2,
        concat_axis=1,
        tiled=True,
    )
    query_delta, key_delta, value_delta = jax.vmap(attend_slot_back)(
        query, key_rows, value_rows, keep_full, log_sums, mixed_delta
    )
    query_back, key_back, value_back = (
        lax.all_to_all(
            query_delta.astype(jnp.bfloat16), "seq", split_axis=1, concat_axis=2, tiled=True
        ),
        lax.all_to_all(
            key_delta.astype(jnp.bfloat16), "seq", split_axis=1, concat_axis=2, tiled=True
        ),
        lax.all_to_all(
            value_delta.astype(jnp.bfloat16), "seq", split_axis=1, concat_axis=2, tiled=True
        ),
    )
    query_plain, key_plain = pull_turn(
        (query_back.astype(jnp.float32), key_back.astype(jnp.float32))
    )
    joined_delta = jnp.stack([query_plain, key_plain, value_back.astype(jnp.float32)], axis=2)
    joined_delta = joined_delta.reshape(row_count, 3 * width).astype(jnp.bfloat16)
    in_delta = transposed_times(first_in, joined_delta)
    in_bias_delta = jnp.sum(joined_delta.astype(jnp.float32), axis=0)
    first_delta = times_transposed(joined_delta, in_matrix).reshape(slot_count, token_count, width)
    source_one, gain_one_delta, shift_one_delta = pull_one(first_delta)
    (
        in_gradient,
        in_bias_gradient,
        out_gradient,
        bias_gradient,
        gain_one_gradient,
        shift_one_gradient,
        gain_two_gradient,
        shift_two_gradient,
    ) = (
        lax.psum_scatter(in_delta, ("fsdp", "seq"), scatter_dimension=0, tiled=True),
        lax.psum_scatter(in_bias_delta, ("fsdp", "seq"), scatter_dimension=0, tiled=True),
        lax.psum_scatter(out_delta, ("fsdp", "seq"), scatter_dimension=0, tiled=True),
        lax.psum_scatter(bias_sum, ("fsdp", "seq"), scatter_dimension=0, tiled=True),
        lax.psum_scatter(gain_one_delta, ("fsdp", "seq"), scatter_dimension=0, tiled=True),
        lax.psum_scatter(shift_one_delta, ("fsdp", "seq"), scatter_dimension=0, tiled=True),
        lax.psum_scatter(gain_two_delta, ("fsdp", "seq"), scatter_dimension=0, tiled=True),
        lax.psum_scatter(shift_two_delta, ("fsdp", "seq"), scatter_dimension=0, tiled=True),
    )
    input_gradient = delta_out + source_one + source_two
    return (
        layer_output,
        input_gradient,
        in_gradient,
        in_bias_gradient,
        out_gradient,
        bias_gradient,
        up_gradient,
        up_bias_gradient,
        down_gradient,
        bias_gradient,
        gain_one_gradient,
        shift_one_gradient,
        gain_two_gradient,
        shift_two_gradient,
    )


def solution(mesh):
    return jax.shard_map(
        local,
        mesh=mesh,
        in_specs=(
            P("fsdp", "seq", None),
            P("fsdp"),
            P("fsdp", "seq", None),
            P(("fsdp", "seq"), None),
            P(("fsdp", "seq")),
            P(("fsdp", "seq"), None),
            P(("fsdp", "seq")),
            P(("fsdp", "seq"), None),
            P(("fsdp", "seq")),
            P(("fsdp", "seq"), None),
            P(("fsdp", "seq")),
            P(("fsdp", "seq")),
            P(("fsdp", "seq")),
            P(("fsdp", "seq")),
            P(("fsdp", "seq")),
        ),
        out_specs=(
            P("fsdp", "seq", None),
            P("fsdp", "seq", None),
            P(("fsdp", "seq"), None),
            P(("fsdp", "seq")),
            P(("fsdp", "seq"), None),
            P(("fsdp", "seq")),
            P(("fsdp", "seq"), None),
            P(("fsdp", "seq")),
            P(("fsdp", "seq"), None),
            P(("fsdp", "seq")),
            P(("fsdp", "seq")),
            P(("fsdp", "seq")),
            P(("fsdp", "seq")),
            P(("fsdp", "seq")),
        ),
        check_vma=False,
    )
```

profile of v0, /device:TPU:0, one launch (start us, length us, event | category | flops | bytes accessed | tf_op | source)
XLA Modules:
  0.0 1959.2 jit_solution(5670677345125691977)
XLA Ops:
  16.4 43.3 %all-reduce.25 = (bf16[6144]{0:T(1024)(128)(2,1)S(1)}, bf16[2048]{0:T(1024)(128)(2,1)S(1)}, bf16[2048]{0:T(1024)(128)(2,1)S(1)}, bf16[2048]{0:T(1024)(128)(2,1)S...) all-reduce(bf16[6144]{0:T(1024)(128)(2,1)S(1)} %dynamic-update-slic, ...), channel_id=1, replica_groups=mesh['fsdp'=8,'seq'=4] {'fsdp','seq'}, use_global_device_ids=true, to_apply=%add.12 | all-reduce | flops 18432 | bytes 73728
  59.7 2.7 fusion.76
  67.0 9.8 all-gather
  76.8 66.3 %all-gather.12.cloned.1.call-done = bf16[1,1024,2048]{2,1,0:T(8,128)(2,1)} async-done(((bf16[1,256,2048]{2,1,0:T(8,128)(2,1)}), bf16[1,1024,2048]{2,1,0:T(8,128)(2,1)}) %all-gather.12.cloned.1.call-update) | async-done | bytes 4194320 | tf_op jit(solution)/shard_map/all_gather | solution.py:243
  143.0 54.8 %all-gather.14.cloned.1.call-done = bf16[2048,2048]{1,0:T(8,128)(2,1)} async-done(((bf16[256,2048]{1,0:T(8,128)(2,1)}), bf16[2048,2048]{1,0:T(8,128)(2,1)}) %all-gather.14.cloned.1.call-update) | async-done | bytes 8388624 | tf_op jit(solution)/shard_map/all_gather | solution.py:239
  197.9 31.6 %multiply_convert_fusion.1 = (bf16[1024,2048]{1,0:T(8,128)(2,1)}, f32[1024,2048]{1,0:T(8,128)}, f32[1024,2048]{1,0:T(8,128)}) fusion(f32[2048]{0:T(1024)S(1)} %bitcast.299, bf16[2048,2048]{1,0:T(8,128)(2,1)} %all-gather.14.cloned.1.call-done, bf16[1,1024,2048]{2,1,0:T(8,128)(2,1)} %all-gather.12.cloned.1.call-done), kind=kOutput, calls=%fused_computation.61 | convolution fusion | flops 8728346624 | bytes 33562624 | tf_op jit(solution)/shard_map/dot_general | solution.py:44
  229.5 50.8 %all-gather.18.cloned.1.call-done = bf16[1,1024,2048]{2,1,0:T(8,128)(2,1)} async-done(((bf16[1,256,2048]{2,1,0:T(8,128)(2,1)}), bf16[1,1024,2048]{2,1,0:T(8,128)(2,1)}) %all-gather.18.cloned.1.call-update) | async-done | bytes 4194320 | tf_op jit(solution)/shard_map/all_gather | solution.py:254
  280.3 54.7 %all-gather.16.cloned.1.call-done = bf16[2048,2048]{1,0:T(8,128)(2,1)} async-done(((bf16[256,2048]{1,0:T(8,128)(2,1)}), bf16[2048,2048]{1,0:T(8,128)(2,1)}) %all-gather.16.cloned.1.call-update) | async-done | bytes 8388624 | tf_op jit(solution)/shard_map/all_gather | solution.py:241
  335.0 19.4 fusion.110
  356.3 12.9 convert_bitcast_fusion
  369.3 14.1 convolution_convert_fusion.1
  383.9 31.2 %all-gather.10.cloned.1.call-done = bf16[2048,2048]{1,0:T(8,128)(2,1)} async-done(((bf16[64,2048]{1,0:T(8,128)(2,1)}), bf16[2048,2048]{1,0:T(8,128)(2,1)}) %all-gather.10.cloned.1.call-update) | async-done | bytes 8388624 | tf_op jit(solution)/shard_map/all_gather | solution.py:188
  415.0 5.7 fusion.88
  422.3 4.7 all-to-all-start.4
  427.0 163.5 %all-gather.8.cloned.1.call-done = bf16[2048,6144]{1,0:T(8,128)(2,1)} async-done(((bf16[64,6144]{1,0:T(8,128)(2,1)}), bf16[2048,6144]{1,0:T(8,128)(2,1)}) %all-gather.8.cloned.1.call-update) | async-done | bytes 25165840 | tf_op jit(solution)/shard_map/all_gather | solution.py:186
  590.5 12.6 fusion.68
  612.8 4.2 all-to-all-start.1
  618.9 53.1 %all-to-all-done.1 = bf16[1,256,16,128]{3,1,0,2:T(8,128)(2,1)} async-done(((bf16[1,256,16,128]{3,1,0,2:T(8,128)(2,1)}), bf16[1,256,16,128]{3,1,0,2:T(8,128)(2,1)}, u32[]{:S(2)}, u32[]{:S(2)}) %all-to-all-start.1) | async-done | bytes 1048608 | tf_op jit(solution)/shard_map/all_to_all | solution.py:219
  672.0 3.9 all-to-all-start
  679.0 33.3 %all-to-all-done = bf16[1,256,16,128]{3,1,0,2:T(8,128)(2,1)S(1)} async-done(((bf16[1,256,16,128]{3,1,0,2:T(8,128)(2,1)}), bf16[1,256,16,128]{3,1,0,2:T(8,128)(2,1)S(1)}, u32[]{:S(2)}, u32[]{:S(2)}) %all-to-all-start) | async-done | bytes 1048608 | tf_op jit(solution)/shard_map/all_to_all | solution.py:216
  712.3 4.3 all-to-all-start.2
  716.6 15.0 convolution_convert_fusion
  736.3 5.7 all-to-all-done.2
  745.4 26.7 %while.31 = (s32[]{:T(128)}, bf16[2,1,512,4,128]{4,2,0,3,1:T(8,128)(2,1)}, f32[2,1,4,512]{3,2,1,0:T(4,128)S(1)}, s32[2]{0:T(128)S(1)}, bf16[1,1024,4,128]{3,1,2,...) while((s32[]{:T(128)}, ...), condition=%wide.region_5.6_spmd.clone, body=%wide.region_2.5_spmd.clone.sunk | while | flops 1099955712 | bytes 35199700 | solution.py:81
  749.7 2.9 fusion.147
  755.1 3.7 fusion.149
  763.1 2.9 fusion.147
  768.4 3.7 fusion.149
  773.2 55.0 %while.32 = (s32[]{:T(128)}, f32[1,1024,4,128]{1,3,2,0:T(8,128)S(1)}, f32[1,1024,4,128]{1,3,2,0:T(8,128)}, bf16[2,1,512,4,128]{4,2,0,3,1:T(8,128)(2,1)}, s32[2]{...) while((s32[]{:T(128)}, ...), condition=%wide.region_9.10_spmd.clone, body=%wide.region_7.9_spmd.clone.sunk | while | flops 2709257728 | bytes 170966912 | solution.py:131
  776.0 2.8 fusion.158
  780.5 3.7 multiply_reduce_fusion.2
  784.3 3.3 copy-done
  790.0 3.8 bitcast_add_fusion.4
  802.9 2.9 fusion.158
  807.5 3.7 multiply_reduce_fusion.2
  811.2 3.5 copy-done
  817.1 3.8 bitcast_add_fusion.4
  824.3 3.9 bitcast_add_fusion.5
  828.2 3.1 copy.149
  831.3 3.5 all-to-all-start.5
  836.5 22.4 %all-to-all-done.5 = bf16[1,1024,4,128]{3,2,0,1:T(4,128)(2,1)S(1)} async-done(((bf16[1,1024,4,128]{3,2,0,1:T(4,128)(2,1)}), bf16[1,1024,4,128]{3,2,0,1:T(4,128)(2,1)S(1)}, u32[]{:S(2)}, u32[]{:S(2)}) %all-to-all-start.5) | async-done | bytes 1048608 | tf_op jit(solution)/shard_map/all_to_all | solution.py:297
  859.9 3.5 all-to-all-start.6
  863.5 14.3 convert_bitcast_fusion.1
  877.8 2.9 copy.154
  880.6 8.0 all-to-all-done.6
  888.6 4.3 all-to-all-start.7
  892.9 3.0 copy.143
  900.6 45.7 %all-to-all-done.7 = bf16[1,1024,4,128]{3,2,0,1:T(4,128)(2,1)} async-done(((bf16[1,1024,4,128]{3,2,0,1:T(4,128)(2,1)}), bf16[1,1024,4,128]{3,2,0,1:T(4,128)(2,1)}, u32[]{:S(2)}, u32[]{:S(2)}) %all-to-all-start.7) | async-done | bytes 1048608 | tf_op jit(solution)/shard_map/all_to_all | solution.py:303
  946.3 3.9 all-to-all-start.3
  958.1 3.4 convert_reduce_fusion
  961.4 4.7 copy.156
  966.1 31.0 %all-to-all-done.3 = bf16[1,1024,4,128]{3,2,0,1:T(4,128)(2,1)S(1)} async-done(((bf16[1,1024,4,128]{3,2,0,1:T(4,128)(2,1)}), bf16[1,1024,4,128]{3,2,0,1:T(4,128)(2,1)S(1)}, u32[]{:S(2)}, u32[]{:S(2)}) %all-to-all-start.3) | async-done | bytes 1048608 | tf_op jit(solution)/shard_map/all_to_all | solution.py:227
  999.8 14.7 fusion.79
  1016.9 3.8 fusion.81
  1020.8 3.4 fusion.86
  1024.3 8.1 fusion.94
  1033.1 21.9 %fusion.103 = f32[2048,6144]{1,0:T(8,128)} fusion(bf16[256,6144]{0,1:T(8,128)(2,1)} %bitcast.282, bf16[1,256,2048]{2,1,0:T(8,128)(2,1)S(1)} %copy-done.4, f32[2048]{0:T(1024)S(1)} %copy-done.31, f32[2048]{0:T(1024)S(1)} %copy-done.29, f32[256]{0:T(256)S(1)} %copy-done.35, f32[256]{0:T(256)S(1)} %copy-done.37), kind=kOutput, calls=%fused_computation.179 | convolution fusion | flops 6445596672 | bytes 54544384 | tf_op jit(solution)/shard_map/dot_general | solution.py:50
  1056.9 13.9 all-reduce.19
  1071.5 2.8 convert_element_type.312
  1074.3 2.8 convert_element_type.315
  1077.1 7.5 fusion.71
  1084.6 62.8 %all-reduce.28.cloned.1.call-done = (f32[6144]{0:T(1024)}, f32[2048]{0:T(1024)}, f32[2048]{0:T(1024)}, f32[2048]{0:T(1024)}, f32[2048]{0:T(1024)}, /*index=5*/f32[2048]{0:T(1024)}) async-done(((f32[6144]{0:T(1024)}, f32[2048]{0:T(1024)}, f32[2048]{0:T(1024)}, f32[2048]{0:T(1024)}, f32[2048]{0:T(1024)}, /*index=5*/f32[2048]{0:T(1024)}), (f32[6144]{0:T(1024)}, f32[2048]{0:T(1024)}, f32[2048]{0:T(1024)}, ...) | async-done | bytes 65552
  1154.5 361.0 %reduce-scatter.13.cloned.1.call-done = f32[64,2048]{1,0:T(8,128)} async-done(((f32[2048,2048]{1,0:T(8,128)}), f32[64,2048]{1,0:T(8,128)}) %reduce-scatter.13.cloned.1.call-update) | async-done | bytes 524304 | tf_op jit(solution)/shard_map/reduce_scatter | solution.py:328
  1515.5 436.4 %reduce-scatter.11.cloned.1.call-done = f32[64,6144]{1,0:T(8,128)} async-done(((f32[2048,6144]{1,0:T(8,128)}), f32[64,6144]{1,0:T(8,128)}) %reduce-scatter.11.cloned.1.call-update) | async-done | bytes 1572880 | tf_op jit(solution)/shard_map/reduce_scatter | solution.py:326
  (259 shorter events, 100.0 us)
Async XLA Ops:
  7.2 135.9 %all-gather.12.cloned.1.call-start = ((), (), s32[]{:S(2)}) async-start(), calls=%async_computation.16 | async-start | bytes 5242880 | tf_op jit(solution)/shard_map/all_gather | solution.py:243
  7.2 56.6 %copy-start.18 = (bf16[1,256,2048]{2,1,0:T(8,128)(2,1)S(1)}, bf16[1,256,2048]{2,1,0:T(8,128)(2,1)}, u32[]{:S(2)}) copy-start(bf16[1,256,2048]{2,1,0:T(8,128)(2,1)} %param.21) | copy-start | bytes 3145732
  8.8 581.7 %copy-start.36 = (f32[256]{0:T(256)}, f32[256]{0:T(256)S(1)}, u32[]{:S(2)}) copy-start(f32[256]{0:T(256)S(1)} %broadcast_multiply_fusion.1) | copy-start | bytes 3076
  10.4 49.2 %copy-start.38 = (f32[256]{0:T(256)}, f32[256]{0:T(256)S(1)}, u32[]{:S(2)}) copy-start(f32[256]{0:T(256)S(1)} %fusion.78) | copy-start | bytes 3076
  10.5 580.0 %copy-start.34 = (f32[256]{0:T(256)}, f32[256]{0:T(256)S(1)}, u32[]{:S(2)}) copy-start(f32[256]{0:T(256)S(1)} %fusion.101) | copy-start | bytes 3076
  59.7 5.4 copy-start.32
  62.4 4.6 copy-start.45
  62.4 135.5 %all-gather.14.cloned.1.call-start = ((), (), s32[]{:S(2)}) async-start(), calls=%async_computation.17 | async-start | bytes 9437184 | tf_op jit(solution)/shard_map/all_gather | solution.py:239
  63.1 217.1 %all-gather.18.cloned.1.call-start = ((), (), s32[]{:S(2)}) async-start(), calls=%async_computation.20 | async-start | bytes 5242880 | tf_op jit(solution)/shard_map/all_gather | solution.py:254
  63.9 3.1 copy-start.40
  65.1 269.8 %all-gather.16.cloned.1.call-start = ((), (), s32[]{:S(2)}) async-start(), calls=%async_computation.18 | async-start | bytes 9437184 | tf_op jit(solution)/shard_map/all_gather | solution.py:241
  65.7 349.3 %all-gather.10.cloned.1.call-start = ((), (), s32[]{:S(2)}) async-start(), calls=%async_computation.15 | async-start | bytes 8650752 | tf_op jit(solution)/shard_map/all_gather | solution.py:188
  66.3 524.2 %all-gather.8.cloned.1.call-start = ((), (), s32[]{:S(2)}) async-start(), calls=%async_computation.14 | async-start | bytes 25952256 | tf_op jit(solution)/shard_map/all_gather | solution.py:186
  66.9 932.8 %reduce-scatter.9.cloned.1.call-start = ((), (), s32[]{:S(2)}) async-start(), calls=%async_computation.21 | async-start | bytes 5242880 | tf_op jit(solution)/shard_map/reduce_scatter | solution.py:260
  369.2 702.3 %reduce-scatter.15.cloned.1.call-start = ((), (), s32[]{:S(2)}) async-start(), calls=%async_computation.24 | async-start | bytes 9437184 | tf_op jit(solution)/shard_map/reduce_scatter | solution.py:267
  383.4 31.6 %copy-start.12 = (bf16[1,256,2048]{2,1,0:T(8,128)(2,1)S(1)}, bf16[1,256,2048]{2,1,0:T(8,128)(2,1)}, u32[]{:S(2)}) copy-start(bf16[1,256,2048]{2,1,0:T(8,128)(2,1)} %fusion.87) | copy-start | bytes 3145732
  383.4 207.1 %copy-start.28 = (f32[2048]{0:T(1024)}, f32[2048]{0:T(1024)S(1)}, u32[]{:S(2)}) copy-start(f32[2048]{0:T(1024)S(1)} %convert_element_type.269) | copy-start | bytes 24580
  383.5 207.1 %copy-start.30 = (f32[2048]{0:T(1024)}, f32[2048]{0:T(1024)S(1)}, u32[]{:S(2)}) copy-start(f32[2048]{0:T(1024)S(1)} %convert_element_type.270) | copy-start | bytes 24580
  383.8 226.1 %copy-start.24 = (f32[256,32]{1,0:T(8,128)}, f32[256,32]{1,0:T(8,128)S(1)}, u32[]{:S(2)}) copy-start(f32[256,32]{1,0:T(8,128)S(1)} %copy.133) | copy-start | bytes 98308
  383.9 226.1 %copy-start.26 = (f32[256,32]{1,0:T(8,128)}, f32[256,32]{1,0:T(8,128)S(1)}, u32[]{:S(2)}) copy-start(f32[256,32]{1,0:T(8,128)S(1)} %copy.134) | copy-start | bytes 98308
  420.8 169.7 %copy-start.3 = (bf16[1,256,2048]{2,1,0:T(8,128)(2,1)S(1)}, bf16[1,256,2048]{2,1,0:T(8,128)(2,1)}, u32[]{:S(2)}) copy-start(bf16[1,256,2048]{2,1,0:T(8,128)(2,1)} %param.19) | copy-start | bytes 3145732
  422.3 190.5 %all-to-all-start.4 = ((bf16[1,256,16,128]{3,1,0,2:T(8,128)(2,1)}), bf16[1,256,16,128]{3,1,0,2:T(8,128)(2,1)}, u32[]{:S(2)}, u32[]{:S(2)}) async-start(bf16[1,256,16,128]{3,1,0,2:T(8,128)(2,1)} %copy.146), calls=%async_computation.5 | async-start | bytes 2097152 | tf_op jit(solution)/shard_map/all_to_all | solution.py:286
  604.2 2.6 copy-start.10
  612.8 59.3 %all-to-all-start.1 = ((bf16[1,256,16,128]{3,1,0,2:T(8,128)(2,1)}), bf16[1,256,16,128]{3,1,0,2:T(8,128)(2,1)}, u32[]{:S(2)}, u32[]{:S(2)}) async-start(bf16[1,256,16,128]{3,1,0,2:T(8,128)(2,1)} %maximum_bitcast_fusion.1), calls=%async_computation.1 | async-start | bytes 2097152 | tf_op jit(solution)/shard_map/all_to_all | solution.py:219
  672.0 40.2 %all-to-all-start = ((bf16[1,256,16,128]{3,1,0,2:T(8,128)(2,1)}), bf16[1,256,16,128]{3,1,0,2:T(8,128)(2,1)S(1)}, u32[]{:S(2)}, u32[]{:S(2)}) async-start(bf16[1,256,16,128]{3,1,0,2:T(8,128)(2,1)} %maximum_bitcast_fusion), calls=%async_computation | async-start | bytes 2097152 | tf_op jit(solution)/shard_map/all_to_all | solution.py:216
  712.2 19.3 copy-start.22
  712.3 29.8 %all-to-all-start.2 = ((bf16[1,256,16,128]{3,1,0,2:T(8,128)(2,1)}), bf16[1,256,16,128]{3,1,0,2:T(8,128)(2,1)}, u32[]{:S(2)}, u32[]{:S(2)}) async-start(bf16[1,256,16,128]{3,1,0,2:T(8,128)(2,1)} %bitcast.288), calls=%async_computation.2 | async-start | bytes 2097152 | tf_op jit(solution)/shard_map/all_to_all | solution.py:222
  716.5 357.7 %reduce-scatter.17.cloned.1.call-start = ((), (), s32[]{:S(2)}) async-start(), calls=%async_computation.25 | async-start | bytes 9437184 | tf_op jit(solution)/shard_map/reduce_scatter | solution.py:273
  731.6 3.7 copy-start.23
  752.7 2.4 copy-start.5
  766.0 2.4 copy-start.5
  776.0 4.6 copy-start.7
  784.3 3.3 copy-start
  790.0 3.9 copy-start.2
  790.0 7.5 copy-start.1
  793.8 4.2 copy-start.6
  802.8 4.7 copy-start.7
  811.2 3.5 copy-start
  817.1 3.9 copy-start.2
  817.1 6.7 copy-start.1
  821.0 3.3 copy-start.6
  831.3 27.6 %all-to-all-start.5 = ((bf16[1,1024,4,128]{3,2,0,1:T(4,128)(2,1)}), bf16[1,1024,4,128]{3,2,0,1:T(4,128)(2,1)S(1)}, u32[]{:S(2)}, u32[]{:S(2)}) async-start(bf16[1,1024,4,128]{3,2,0,1:T(4,128)(2,1)} %copy.149), calls=%async_computation.6 | async-start | bytes 2097152 | tf_op jit(solution)/shard_map/all_to_all | solution.py:297
  859.9 28.8 %all-to-all-start.6 = ((bf16[1,1024,4,128]{3,2,0,1:T(4,128)(2,1)}), bf16[1,1024,4,128]{3,2,0,1:T(4,128)(2,1)S(1)}, u32[]{:S(2)}, u32[]{:S(2)}) async-start(bf16[1,1024,4,128]{3,2,0,1:T(4,128)(2,1)} %copy.152), calls=%async_computation.7 | async-start | bytes 2097152 | tf_op jit(solution)/shard_map/all_to_all | solution.py:300
  863.4 213.6 %reduce-scatter.7.cloned.1.call-start = ((), (), s32[]{:S(2)}) async-start(), calls=%async_computation.19 | async-start | bytes 5242880 | tf_op jit(solution)/shard_map/reduce_scatter | solution.py:247
  877.7 18.2 copy-start.21
  888.6 57.6 %all-to-all-start.7 = ((bf16[1,1024,4,128]{3,2,0,1:T(4,128)(2,1)}), bf16[1,1024,4,128]{3,2,0,1:T(4,128)(2,1)}, u32[]{:S(2)}, u32[]{:S(2)}) async-start(bf16[1,1024,4,128]{3,2,0,1:T(4,128)(2,1)} %copy.154), calls=%async_computation.8 | async-start | bytes 2097152 | tf_op jit(solution)/shard_map/all_to_all | solution.py:303
  900.6 51.2 %copy-start.27 = (f32[256,32]{1,0:T(8,128)S(1)}, f32[256,32]{1,0:T(8,128)}, u32[]{:S(2)}) copy-start(f32[256,32]{1,0:T(8,128)} %copy-done.26) | copy-start | bytes 98308
  946.3 50.8 %all-to-all-start.3 = ((bf16[1,1024,4,128]{3,2,0,1:T(4,128)(2,1)}), bf16[1,1024,4,128]{3,2,0,1:T(4,128)(2,1)S(1)}, u32[]{:S(2)}, u32[]{:S(2)}) async-start(bf16[1,1024,4,128]{3,2,0,1:T(4,128)(2,1)} %copy.143), calls=%async_computation.3 | async-start | bytes 2097152 | tf_op jit(solution)/shard_map/all_to_all | solution.py:227
  950.2 197.1 %all-reduce.28.cloned.1.call-start = ((), (), s32[]{:S(2)}) async-start(), calls=%async_computation.26 | async-start | bytes 131072
  966.1 33.6 %copy-start.4 = (bf16[1,256,2048]{2,1,0:T(8,128)(2,1)S(1)}, bf16[1,256,2048]{2,1,0:T(8,128)(2,1)}, u32[]{:S(2)}) copy-start(bf16[1,256,2048]{2,1,0:T(8,128)(2,1)} %param.19) | copy-start | bytes 3145732
  966.1 33.6 %copy-start.29 = (f32[2048]{0:T(1024)S(1)}, f32[2048]{0:T(1024)}, u32[]{:S(2)}) copy-start(f32[2048]{0:T(1024)} %copy-done.28) | copy-start | bytes 24580
  966.1 33.6 %copy-start.33 = (f32[2048]{0:T(1024)S(1)}, f32[2048]{0:T(1024)}, u32[]{:S(2)}) copy-start(f32[2048]{0:T(1024)} %copy-done.32) | copy-start | bytes 24580
  966.1 33.6 %copy-start.37 = (f32[256]{0:T(256)S(1)}, f32[256]{0:T(256)}, u32[]{:S(2)}) copy-start(f32[256]{0:T(256)} %copy-done.36) | copy-start | bytes 3076
  999.8 17.1 copy-start.39
  999.8 17.1 copy-start.16
  999.8 17.1 copy-start.35
  1014.6 6.2 copy-start.41
  1016.9 3.9 copy-start.11
  1016.9 3.9 copy-start.17
  1016.9 3.9 copy-start.19
  1020.8 3.5 copy-start.13
  1024.2 491.2 %reduce-scatter.13.cloned.1.call-start = ((), (), s32[]{:S(2)}) async-start(), calls=%async_computation.23 | async-start | bytes 17301504 | tf_op jit(solution)/shard_map/reduce_scatter | solution.py:328
  1032.4 919.5 %reduce-scatter.11.cloned.1.call-start = ((), (), s32[]{:S(2)}) async-start(), calls=%async_computation.22 | async-start | bytes 51904512 | tf_op jit(solution)/shard_map/reduce_scatter | solution.py:326
  1148.1 804.3 %copy-start.47 = (f32[64]{0:T(128)}, f32[64]{0:T(128)S(1)}, u32[]{:S(2)}) copy-start(f32[64]{0:T(128)S(1)} %dynamic-slice.16) | copy-start | bytes 772
  (12 other events, 15.7 us)
Sparse Core Ops, SparseCore 0:
  62.5 80.5 all-gather.11
  144.9 52.9 all-gather.13
  199.5 80.7 all-gather.17
  282.0 52.9 all-gather.15
  337.7 77.2 all-gather.9
  417.8 172.6 all-gather.7
  592.8 99.6 reduce-scatter.8
  696.4 88.4 reduce-scatter.14
  788.3 71.2 reduce-scatter.16
  877.9 111.9 reduce-scatter.6
  1024.4 122.9 all-reduce.27
  1150.1 365.3 reduce-scatter.12
  1522.5 429.3 reduce-scatter.10
where the time goes:
time: 1960 us
  waiting for transfers between devices  1480 us (76%)
  matrix products  222 us (11%)
  local copies, waits for them, and re-layouts  76 us (4%)
  blocking collectives  66.9 us (3%)
  other arithmetic  53.9 us (3%)
  starting transfers between devices  32.8 us (2%)
    reduce_scatter x1, waiting for transfers between devices, local(): lax.psum_scatter(in_delta, ('fsdp', 'seq'), scatter_dimension=0, tiled=True)  436 us
    reduce_scatter x1, waiting for transfers between devices, local(): lax.psum_scatter(out_delta, ('fsdp', 'seq'), scatter_dimension=0, tiled=T...  361 us
    all_gather x1, waiting for transfers between devices, local(): lax.all_gather(in_weight, ('fsdp', 'seq'), axis=0, tiled=True)  164 us
    dot_general x4, matrix products, times_transposed(): lax.dot_general(left_side, right_side, (((1,), (1,)), ((), ())), preferre...  71.4 us
    all_gather x1, waiting for transfers between devices, local(): lax.all_gather(second_in, 'seq', axis=1, tiled=True)  66.3 us
    unnamed x14, waiting for transfers between devices  65.2 us
    dot_general x4, matrix products, transposed_times(): lax.dot_general(left_side, right_side, (((0,), (0,)), ((), ())), preferre...  59.1 us
    unnamed x2, blocking collectives  57.1 us
  transfers between devices with their start and end apart: 21, of which 16 were waited for; matrix products, arithmetic and copies ran while one was open for 16% of the time, Pallas kernels for 0%

commit v1 on v0

--- a/solution.py
+++ b/solution.py
@@ -8,6 +8,28 @@
 ROT = 32
 EPSILON = 1e-05
 MASKED_SCORE = -1e30
+
+
+def in_order(blocks, dim):
+    lengths = list(blocks.shape[1:])
+    lengths[dim] *= blocks.shape[0]
+    return jnp.moveaxis(blocks, 0, dim).reshape(lengths)
+
+
+def ring_gather(x, axis, dim):
+    size = lax.axis_size(axis)
+    pairs = [(i, (i + 1) % size) for i in range(size)]
+    back = [(b, a) for a, b in pairs]
+    lower, upper = ([], [])
+    for step in range(size - 1):
+        if step % 2 == 0:
+            lower.append(lax.ppermute(lower[-1] if lower else x, axis, pairs))
+        else:
+            upper.append(lax.ppermute(upper[-1] if upper else x, axis, back))
+    blocks = jnp.stack([*lower[::-1], x, *upper])
+    shift = lax.axis_index(axis) - len(lower)
+    blocks = blocks[(jnp.arange(size) - shift) % size]
+    return in_order(blocks, dim)
 
 
 def layer_norm(values, norm_gain, norm_shift):
@@ -236,7 +258,7 @@
     delta_low = delta_out.astype(jnp.bfloat16)
     delta_rows = delta_low.reshape(row_count, width)
     up_matrix, up_offset, down_matrix = (
-        lax.all_gather(up_weight, "fsdp", axis=0, tiled=True),
+        ring_gather(up_weight, "fsdp", 0),
         lax.all_gather(up_bias, "fsdp", axis=0, tiled=True),
         lax.all_gather(down_weight, "fsdp", axis=0, tiled=True),
     )

time: 1960 us -> 1890 us (0.964)
  waiting for transfers between devices: 1480 us -> 1390 us
    all_gather x1, waiting for transfers between devices: 66.3 us -> 0.01 us  [local(): lax.all_gather(second_in, 'seq', axis=1, tiled=True)]
    ppermute x0 -> x7, waiting for transfers between devices: none -> 63.4 us  [the longest x4 62.1 us: ring_gather(): lower.append(lax.ppermute(lower[-1] if lower else x, axis, pairs))]
    all_gather x1 -> x0, waiting for transfers between devices: 54.8 us -> none  [local(): lax.all_gather(up_weight, 'fsdp', axis=0, tiled=True)]
    all_to_all x1, waiting for transfers between devices: 53.1 us -> 6.23 us  [local(): lax.all_to_all(turned[1].astype(jnp.bfloat16), 'seq', split_axis=2, conca...]
    all_to_all x1, waiting for transfers between devices: 5.68 us -> 47.4 us  [local(): lax.all_to_all(joined[:, :, 2].astype(jnp.bfloat16), 'seq', split_axis=2,...]
    all_gather x1, waiting for transfers between devices: 50.8 us -> 18.6 us  [local(): lax.all_gather(delta_low, 'seq', axis=1, tiled=True)]
    unnamed x14 -> x13, waiting for transfers between devices: 65.2 us -> 62.3 us
  transfers between devices with their start and end apart: 21 -> 27, of which waited for: 16 -> 18; matrix products, arithmetic and copies ran while one was open for 16% -> 18% of each run, Pallas kernels for 0% -> 0%
where the time goes in v1:
time: 1890 us; the launch traced here: 1880 us
  waiting for transfers between devices  1390 us (74%)
  matrix products  213 us (11%)
  local copies, waits for them, and re-layouts  90.6 us (5%)
  blocking collectives  71.6 us (4%)
  other arithmetic  49.1 us (3%)
  starting transfers between devices  38.4 us (2%)
    reduce_scatter x1, waiting for transfers between devices, local(): lax.psum_scatter(in_delta, ('fsdp', 'seq'), scatter_dimension=0, tiled=True)  436 us
    reduce_scatter x1, waiting for transfers between devices, local(): lax.psum_scatter(out_delta, ('fsdp', 'seq'), scatter_dimension=0, tiled=T...  361 us
    all_gather x1, waiting for transfers between devices, local(): lax.all_gather(in_weight, ('fsdp', 'seq'), axis=0, tiled=True)  165 us
    dot_general x4, matrix products, times_transposed(): lax.dot_general(left_side, right_side, (((1,), (1,)), ((), ())), preferre...  72.3 us
    unnamed x13, waiting for transfers between devices  62.3 us
    ppermute x4, waiting for transfers between devices, ring_gather(): lower.append(lax.ppermute(lower[-1] if lower else x, axis, pairs))  62.1 us
    dot_general x4, matrix products, transposed_times(): lax.dot_general(left_side, right_side, (((0,), (0,)), ((), ())), preferre...  59.9 us
    unnamed x2, blocking collectives  55.1 us
  transfers between devices with their start and end apart: 27, of which 18 were waited for; matrix products, arithmetic and copies ran while one was open for 18% of the time, Pallas kernels for 0%

profile of v1, /device:TPU:0, one launch (start us, length us, event | category | flops | bytes accessed | tf_op | source)
XLA Modules:
  0.0 1882.0 jit_solution(5119229594335098638)
XLA Ops:
  16.4 43.2 %all-reduce.25 = (bf16[6144]{0:T(1024)(128)(2,1)S(1)}, bf16[2048]{0:T(1024)(128)(2,1)S(1)}, bf16[2048]{0:T(1024)(128)(2,1)S(1)}, bf16[2048]{0:T(1024)(128)(2,1)S...) all-reduce(bf16[6144]{0:T(1024)(128)(2,1)S(1)} %dynamic-update-slic, ...), channel_id=1, replica_groups=mesh['fsdp'=8,'seq'=4] {'fsdp','seq'}, use_global_device_ids=true, to_apply=%add.12 | all-reduce | flops 18432 | bytes 73728
  60.3 2.7 fusion.76
  67.0 15.1 collective-permute-done
  82.1 2.6 collective-permute-start.4
  84.8 23.4 %collective-permute-done.1 = bf16[256,2048]{1,0:T(8,128)(2,1)S(1)} collective-permute-done((bf16[256,2048]{1,0:T(8,128)(2,1)S(1)}, bf16[256,2048]{1,0:T(8,128)(2,1)S(1)}, u32[]{:S(2)}, u32[]{:S(2)}) %collective-permute-start.1) | collective-permute-done | bytes 1048608 | tf_op jit(solution)/shard_map/ppermute | solution.py:26
  110.8 23.6 %collective-permute-done.2 = bf16[256,2048]{1,0:T(8,128)(2,1)} collective-permute-done((bf16[256,2048]{1,0:T(8,128)(2,1)S(1)}, bf16[256,2048]{1,0:T(8,128)(2,1)}, u32[]{:S(2)}, u32[]{:S(2)}) %collective-permute-start.2) | collective-permute-done | bytes 1048608 | tf_op jit(solution)/shard_map/ppermute | solution.py:26
  134.5 16.5 all-gather
  152.6 2.4 bitcast_dynamic-update-slice_fusion.8
  166.3 8.1 gather_fusion
  174.4 31.6 %multiply_convert_fusion.1 = (bf16[1024,2048]{1,0:T(8,128)(2,1)}, f32[1024,2048]{1,0:T(8,128)}, f32[1024,2048]{1,0:T(8,128)}) fusion(f32[2048]{0:T(1024)S(1)} %bitcast.321, bf16[2048,2048]{1,0:T(8,128)(2,1)} %bitcast.304, bf16[1,1024,2048]{2,1,0:T(8,128)(2,1)} %all-gather.11.cloned.1.call-done), kind=kOutput, calls=%fused_computation.62 | convolution fusion | flops 8728346624 | bytes 33562624 | tf_op jit(solution)/shard_map/dot_general | solution.py:66
  206.0 18.6 all-gather.15.cloned.1.call-done
  224.6 54.8 %all-gather.13.cloned.1.call-done = bf16[2048,2048]{1,0:T(8,128)(2,1)} async-done(((bf16[256,2048]{1,0:T(8,128)(2,1)}), bf16[2048,2048]{1,0:T(8,128)(2,1)}) %all-gather.13.cloned.1.call-update) | async-done | bytes 8388624 | tf_op jit(solution)/shard_map/all_gather | solution.py:263
  279.5 21.0 %fusion.112 = (bf16[2048]{0:T(1024)(128)(2,1)}, bf16[1024,2048]{1,0:T(8,128)(2,1)}) fusion(f32[1024,2048]{1,0:T(8,128)} %get-tuple-element.290, bf16[2048,2048]{1,0:T(8,128)(2,1)} %all-gather.13.cloned.1.call-done, bf16[1,1024,2048]{2,1,0:T(8,128)(2,1)} %all-gather.15.cloned.1.call-done, f32[1024,2048]{1,0:T(8,128)} %get-tuple-element.315, ...), kind=kOutput, calls=%fused_computation.199 | convolution fusion | flops 8623486976 | bytes 33566720 | tf_op jit(solution)/shard_map/dot_general | solution.py:66
  300.5 12.2 convert_bitcast_fusion
  312.8 14.5 convolution_convert_fusion
  327.7 31.8 %all-gather.9.cloned.1.call-done = bf16[2048,2048]{1,0:T(8,128)(2,1)} async-done(((bf16[64,2048]{1,0:T(8,128)(2,1)}), bf16[2048,2048]{1,0:T(8,128)(2,1)}) %all-gather.9.cloned.1.call-update) | async-done | bytes 8388624 | tf_op jit(solution)/shard_map/all_gather | solution.py:210
  359.5 5.7 fusion.88
  366.8 3.5 all-to-all-start.4
  370.3 164.8 %all-gather.7.cloned.1.call-done = bf16[2048,6144]{1,0:T(8,128)(2,1)} async-done(((bf16[64,6144]{1,0:T(8,128)(2,1)}), bf16[2048,6144]{1,0:T(8,128)(2,1)}) %all-gather.7.cloned.1.call-update) | async-done | bytes 25165840 | tf_op jit(solution)/shard_map/all_gather | solution.py:208
  535.2 12.6 fusion.68
  551.9 4.4 all-to-all-start.2
  556.3 2.9 copy_bitcast_fusion
  563.9 47.4 %all-to-all-done.2 = bf16[1,256,16,128]{3,1,0,2:T(8,128)(2,1)} async-done(((bf16[1,256,16,128]{3,1,0,2:T(8,128)(2,1)}), bf16[1,256,16,128]{3,1,0,2:T(8,128)(2,1)}, u32[]{:S(2)}, u32[]{:S(2)}) %all-to-all-start.2) | async-done | bytes 1048608 | tf_op jit(solution)/shard_map/all_to_all | solution.py:244
  611.3 4.2 all-to-all-start
  619.1 37.8 %all-to-all-done = bf16[1,256,16,128]{3,1,0,2:T(8,128)(2,1)} async-done(((bf16[1,256,16,128]{3,1,0,2:T(8,128)(2,1)}), bf16[1,256,16,128]{3,1,0,2:T(8,128)(2,1)}, u32[]{:S(2)}, u32[]{:S(2)}) %all-to-all-start) | async-done | bytes 1048608 | tf_op jit(solution)/shard_map/all_to_all | solution.py:238
  656.9 4.2 all-to-all-start.1
  661.2 14.1 convolution_convert_fusion.1
  681.2 6.2 all-to-all-done.1
  690.9 28.6 %while.31 = (s32[]{:T(128)}, bf16[2,1,512,4,128]{4,2,0,3,1:T(8,128)(2,1)}, f32[2,1,4,512]{3,2,1,0:T(4,128)S(1)}, s32[2]{0:T(128)S(1)}, bf16[1,1024,4,128]{3,1,2,...) while((s32[]{:T(128)}, ...), condition=%wide.region_5.6_spmd.clone, body=%wide.region_2.5_spmd.clone.sunk | while | flops 1099955712 | bytes 39393536 | solution.py:103
  695.2 3.3 fusion.149
  700.8 3.3 fusion.151
  709.4 3.3 fusion.149
  712.7 2.4 fusion.150
  715.1 3.3 fusion.151
  720.5 34.5 %while.32 = (s32[]{:T(128)}, f32[1,1024,4,128]{1,3,2,0:T(8,128)S(1)}, f32[1,1024,4,128]{1,3,2,0:T(8,128)}, bf16[2,1,512,4,128]{4,2,0,3,1:T(8,128)(2,1)}, s32[2]{...) while((s32[]{:T(128)}, ...), condition=%wide.region_9.10_spmd.clone, body=%wide.region_7.9_spmd.clone.sunk | while | flops 2709257728 | bytes 116441008 | solution.py:153
  725.3 2.5 fusion.160
  727.8 3.7 multiply_reduce_fusion.2
  742.0 2.6 fusion.160
  744.7 3.7 multiply_reduce_fusion.2
  755.1 3.0 copy.149
  758.1 3.5 all-to-all-start.5
  761.6 3.0 copy.143
  764.6 22.4 %all-to-all-done.5 = bf16[1,1024,4,128]{3,2,0,1:T(4,128)(2,1)S(1)} async-done(((bf16[1,1024,4,128]{3,2,0,1:T(4,128)(2,1)}), bf16[1,1024,4,128]{3,2,0,1:T(4,128)(2,1)S(1)}, u32[]{:S(2)}, u32[]{:S(2)}) %all-to-all-start.5) | async-done | bytes 1048608 | tf_op jit(solution)/shard_map/all_to_all | solution.py:319
  787.0 4.2 all-to-all-start.3
  793.0 23.6 %all-to-all-done.3 = bf16[1,1024,4,128]{3,2,0,1:T(4,128)(2,1)} async-done(((bf16[1,1024,4,128]{3,2,0,1:T(4,128)(2,1)}), bf16[1,1024,4,128]{3,2,0,1:T(4,128)(2,1)}, u32[]{:S(2)}, u32[]{:S(2)}) %all-to-all-start.3) | async-done | bytes 1048608 | tf_op jit(solution)/shard_map/all_to_all | solution.py:249
  816.5 3.5 all-to-all-start.6
  820.1 13.9 convert_bitcast_fusion.1
  837.3 16.4 all-to-all-done.6
  853.7 4.3 all-to-all-start.7
  862.9 47.5 %all-to-all-done.7 = bf16[1,1024,4,128]{3,2,0,1:T(4,128)(2,1)} async-done(((bf16[1,1024,4,128]{3,2,0,1:T(4,128)(2,1)}), bf16[1,1024,4,128]{3,2,0,1:T(4,128)(2,1)}, u32[]{:S(2)}, u32[]{:S(2)}) %all-to-all-start.7) | async-done | bytes 1048608 | tf_op jit(solution)/shard_map/all_to_all | solution.py:325
  919.9 3.1 convert_reduce_fusion
  923.0 4.7 copy.156
  927.8 13.9 fusion.79
  942.5 3.8 fusion.81
  946.3 3.4 fusion.86
  949.8 9.6 fusion.94
  960.1 21.7 %fusion.105 = f32[2048,6144]{1,0:T(8,128)} fusion(bf16[256,6144]{0,1:T(8,128)(2,1)} %bitcast.301, bf16[1,256,2048]{2,1,0:T(8,128)(2,1)S(1)} %copy-done.4, f32[2048]{0:T(1024)S(1)} %copy-done.34, f32[2048]{0:T(1024)S(1)} %copy-done.32, f32[256]{0:T(256)S(1)} %copy-done.38, f32[256]{0:T(256)S(1)} %copy-done.40), kind=kOutput, calls=%fused_computation.195 | convolution fusion | flops 6445596672 | bytes 54544384 | tf_op jit(solution)/shard_map/dot_general | solution.py:72
  983.7 11.9 all-reduce.19
  996.2 2.8 convert_element_type.315
  999.0 2.8 convert_element_type.312
  1001.8 7.5 fusion.71
  1009.4 60.4 %all-reduce.28.cloned.1.call-done = (f32[6144]{0:T(1024)}, f32[2048]{0:T(1024)}, f32[2048]{0:T(1024)}, f32[2048]{0:T(1024)}, f32[2048]{0:T(1024)}, /*index=5*/f32[2048]{0:T(1024)}) async-done(((f32[6144]{0:T(1024)}, f32[2048]{0:T(1024)}, f32[2048]{0:T(1024)}, f32[2048]{0:T(1024)}, f32[2048]{0:T(1024)}, /*index=5*/f32[2048]{0:T(1024)}), (f32[6144]{0:T(1024)}, f32[2048]{0:T(1024)}, f32[2048]{0:T(1024)}, ...) | async-done | bytes 65552
  1076.9 361.2 %reduce-scatter.13.cloned.1.call-done = f32[64,2048]{1,0:T(8,128)} async-done(((f32[2048,2048]{1,0:T(8,128)}), f32[64,2048]{1,0:T(8,128)}) %reduce-scatter.13.cloned.1.call-update) | async-done | bytes 524304 | tf_op jit(solution)/shard_map/reduce_scatter | solution.py:350
  1438.1 436.3 %reduce-scatter.11.cloned.1.call-done = f32[64,6144]{1,0:T(8,128)} async-done(((f32[2048,6144]{1,0:T(8,128)}), f32[64,6144]{1,0:T(8,128)}) %reduce-scatter.11.cloned.1.call-update) | async-done | bytes 1572880 | tf_op jit(solution)/shard_map/reduce_scatter | solution.py:348
  (291 shorter events, 109.9 us)
Async XLA Ops:
  7.2 56.6 %copy-start.14 = (bf16[1,256,2048]{2,1,0:T(8,128)(2,1)S(1)}, bf16[1,256,2048]{2,1,0:T(8,128)(2,1)}, u32[]{:S(2)}) copy-start(bf16[1,256,2048]{2,1,0:T(8,128)(2,1)} %param.21) | copy-start | bytes 3145732
  7.2 167.2 %all-gather.11.cloned.1.call-start = ((), (), s32[]{:S(2)}) async-start(), calls=%async_computation.16 | async-start | bytes 5242880 | tf_op jit(solution)/shard_map/all_gather | solution.py:265
  8.8 526.4 %copy-start.39 = (f32[256]{0:T(256)}, f32[256]{0:T(256)S(1)}, u32[]{:S(2)}) copy-start(f32[256]{0:T(256)S(1)} %broadcast_multiply_fusion.1) | copy-start | bytes 3076
  10.4 4.3 copy-start.41
  10.4 524.7 %copy-start.37 = (f32[256]{0:T(256)}, f32[256]{0:T(256)S(1)}, u32[]{:S(2)}) copy-start(f32[256]{0:T(256)S(1)} %fusion.101) | copy-start | bytes 3076
  60.3 6.7 copy-start.28
  60.3 74.2 %copy-start.48 = (bf16[256]{0:T(256)(128)(2,1)S(1)}, bf16[256]{0:T(256)(128)(2,1)}, u32[]{:S(2)}) copy-start(bf16[256]{0:T(256)(128)(2,1)} %param.27) | copy-start | bytes 1540
  63.0 161.6 %all-gather.15.cloned.1.call-start = ((), (), s32[]{:S(2)}) async-start(), calls=%async_computation.19 | async-start | bytes 5242880 | tf_op jit(solution)/shard_map/all_gather | solution.py:276
  63.8 70.7 %copy-start.43 = (pred[256]{0:T(512)(128)(4,1)}, pred[256]{0:T(512)(128)(4,1)S(1)}, u32[]{:S(2)}) copy-start(pred[256]{0:T(512)(128)(4,1)S(1)} %fusion.100) | copy-start | bytes 772
  65.0 214.4 %all-gather.13.cloned.1.call-start = ((), (), s32[]{:S(2)}) async-start(), calls=%async_computation.17 | async-start | bytes 9437184 | tf_op jit(solution)/shard_map/all_gather | solution.py:263
  65.7 293.8 %all-gather.9.cloned.1.call-start = ((), (), s32[]{:S(2)}) async-start(), calls=%async_computation.15 | async-start | bytes 8650752 | tf_op jit(solution)/shard_map/all_gather | solution.py:210
  66.3 468.9 %all-gather.7.cloned.1.call-start = ((), (), s32[]{:S(2)}) async-start(), calls=%async_computation.14 | async-start | bytes 25952256 | tf_op jit(solution)/shard_map/all_gather | solution.py:208
  66.9 860.9 %reduce-scatter.9.cloned.1.call-start = ((), (), s32[]{:S(2)}) async-start(), calls=%async_computation.20 | async-start | bytes 5242880 | tf_op jit(solution)/shard_map/reduce_scatter | solution.py:282
  67.0 15.2 collective-permute-start
  82.1 26.0 %collective-permute-start.1 = (bf16[256,2048]{1,0:T(8,128)(2,1)S(1)}, bf16[256,2048]{1,0:T(8,128)(2,1)S(1)}, u32[]{:S(2)}, u32[]{:S(2)}) collective-permute-start(bf16[256,2048]{1,0:T(8,128)(2,1)S(1)} %collective-permute-done), channel_id=1, source_target_pairs={{0,4},{4,8},{8,12},{12,16},{16,20},{20,24},{24,28},{28,0},{1,5},{5... | collective-permute-start | bytes 3145736 | tf_op jit(solution)/shard_map/ppermute | solution.py:26
  82.1 26.0 %collective-permute-start.4 = (bf16[256,2048]{1,0:T(8,128)(2,1)S(1)}, bf16[256,2048]{1,0:T(8,128)(2,1)S(1)}, u32[]{:S(2)}, u32[]{:S(2)}) collective-permute-start(bf16[256,2048]{1,0:T(8,128)(2,1)S(1)} %copy-done.28), channel_id=1, source_target_pairs={{4,0},{8,4},{12,8},{16,12},{20,16},{24,20},{28,24},{0,28},{5,1},{9... | collective-permute-start | bytes 3145736 | tf_op jit(solution)/shard_map/ppermute | solution.py:28
  108.2 26.3 %collective-permute-start.2 = (bf16[256,2048]{1,0:T(8,128)(2,1)S(1)}, bf16[256,2048]{1,0:T(8,128)(2,1)}, u32[]{:S(2)}, u32[]{:S(2)}) collective-permute-start(bf16[256,2048]{1,0:T(8,128)(2,1)S(1)} %collective-permute-done.1), channel_id=1, source_target_pairs={{0,4},{4,8},{8,12},{12,16},{16,20},{20,24},{24,28},{28,0},{1,5},{5... | collective-permute-start | bytes 3145736 | tf_op jit(solution)/shard_map/ppermute | solution.py:26
  109.1 41.9 %collective-permute-start.5 = (bf16[256,2048]{1,0:T(8,128)(2,1)S(1)}, bf16[256,2048]{1,0:T(8,128)(2,1)}, u32[]{:S(2)}, u32[]{:S(2)}) collective-permute-start(bf16[256,2048]{1,0:T(8,128)(2,1)S(1)} %collective-permute-done.4), channel_id=1, source_target_pairs={{4,0},{8,4},{12,8},{16,12},{20,16},{24,20},{28,24},{0,28},{5,1},{9... | collective-permute-start | bytes 3145736 | tf_op jit(solution)/shard_map/ppermute | solution.py:28
  134.5 18.2 collective-permute-start.3
  151.0 6.4 copy-start.30
  151.1 14.2 collective-permute-start.6
  279.5 21.1 %copy-start.12 = (bf16[8,256,2048]{2,1,0:T(8,128)(2,1)S(1)}, bf16[8,256,2048]{2,1,0:T(8,128)(2,1)}, u32[]{:S(2)}) copy-start(bf16[8,256,2048]{2,1,0:T(8,128)(2,1)} %gather_fusion) | copy-start | bytes 25165828
  312.7 683.5 %reduce-scatter.17.cloned.1.call-start = ((), (), s32[]{:S(2)}) async-start(), calls=%async_computation.24 | async-start | bytes 9437184 | tf_op jit(solution)/shard_map/reduce_scatter | solution.py:295
  327.3 32.3 %copy-start.11 = (bf16[1,256,2048]{2,1,0:T(8,128)(2,1)S(1)}, bf16[1,256,2048]{2,1,0:T(8,128)(2,1)}, u32[]{:S(2)}) copy-start(bf16[1,256,2048]{2,1,0:T(8,128)(2,1)} %fusion.87) | copy-start | bytes 3145732
  327.3 207.9 %copy-start.31 = (f32[2048]{0:T(1024)}, f32[2048]{0:T(1024)S(1)}, u32[]{:S(2)}) copy-start(f32[2048]{0:T(1024)S(1)} %convert_element_type.269) | copy-start | bytes 24580
  327.3 207.9 %copy-start.33 = (f32[2048]{0:T(1024)}, f32[2048]{0:T(1024)S(1)}, u32[]{:S(2)}) copy-start(f32[2048]{0:T(1024)S(1)} %convert_element_type.270) | copy-start | bytes 24580
  327.6 233.4 %copy-start.24 = (f32[256,32]{1,0:T(8,128)}, f32[256,32]{1,0:T(8,128)S(1)}, u32[]{:S(2)}) copy-start(f32[256,32]{1,0:T(8,128)S(1)} %copy.133) | copy-start | bytes 98308
  327.7 233.3 %copy-start.26 = (f32[256,32]{1,0:T(8,128)}, f32[256,32]{1,0:T(8,128)S(1)}, u32[]{:S(2)}) copy-start(f32[256,32]{1,0:T(8,128)S(1)} %copy.134) | copy-start | bytes 98308
  365.3 169.9 %copy-start.3 = (bf16[1,256,2048]{2,1,0:T(8,128)(2,1)S(1)}, bf16[1,256,2048]{2,1,0:T(8,128)(2,1)}, u32[]{:S(2)}) copy-start(bf16[1,256,2048]{2,1,0:T(8,128)(2,1)} %param.19) | copy-start | bytes 3145732
  366.8 185.1 %all-to-all-start.4 = ((bf16[1,256,16,128]{3,1,0,2:T(8,128)(2,1)}), bf16[1,256,16,128]{3,1,0,2:T(8,128)(2,1)S(1)}, u32[]{:S(2)}, u32[]{:S(2)}) async-start(bf16[1,256,16,128]{3,1,0,2:T(8,128)(2,1)} %copy.146), calls=%async_computation.5 | async-start | bytes 2097152 | tf_op jit(solution)/shard_map/all_to_all | solution.py:308
  551.9 7.3 copy-start.16
  551.9 59.4 %all-to-all-start.2 = ((bf16[1,256,16,128]{3,1,0,2:T(8,128)(2,1)}), bf16[1,256,16,128]{3,1,0,2:T(8,128)(2,1)}, u32[]{:S(2)}, u32[]{:S(2)}) async-start(bf16[1,256,16,128]{3,1,0,2:T(8,128)(2,1)} %bitcast.309), calls=%async_computation.2 | async-start | bytes 2097152 | tf_op jit(solution)/shard_map/all_to_all | solution.py:244
  611.3 45.6 %all-to-all-start = ((bf16[1,256,16,128]{3,1,0,2:T(8,128)(2,1)}), bf16[1,256,16,128]{3,1,0,2:T(8,128)(2,1)}, u32[]{:S(2)}, u32[]{:S(2)}) async-start(bf16[1,256,16,128]{3,1,0,2:T(8,128)(2,1)} %maximum_bitcast_fusion), calls=%async_computation | async-start | bytes 2097152 | tf_op jit(solution)/shard_map/all_to_all | solution.py:238
  656.9 30.6 %all-to-all-start.1 = ((bf16[1,256,16,128]{3,1,0,2:T(8,128)(2,1)}), bf16[1,256,16,128]{3,1,0,2:T(8,128)(2,1)}, u32[]{:S(2)}, u32[]{:S(2)}) async-start(bf16[1,256,16,128]{3,1,0,2:T(8,128)(2,1)} %maximum_bitcast_fusion.1), calls=%async_computation.1 | async-start | bytes 2097152 | tf_op jit(solution)/shard_map/all_to_all | solution.py:241
  661.1 337.9 %reduce-scatter.15.cloned.1.call-start = ((), (), s32[]{:S(2)}) async-start(), calls=%async_computation.23 | async-start | bytes 9437184 | tf_op jit(solution)/shard_map/reduce_scatter | solution.py:289
  725.2 2.5 copy-start.6
  725.2 2.5 copy-start.8
  734.8 2.9 copy-start.1
  742.0 2.7 copy-start.6
  742.0 2.6 copy-start.8
  752.2 2.9 copy-start.1
  758.1 28.9 %all-to-all-start.5 = ((bf16[1,1024,4,128]{3,2,0,1:T(4,128)(2,1)}), bf16[1,1024,4,128]{3,2,0,1:T(4,128)(2,1)S(1)}, u32[]{:S(2)}, u32[]{:S(2)}) async-start(bf16[1,1024,4,128]{3,2,0,1:T(4,128)(2,1)} %copy.149), calls=%async_computation.6 | async-start | bytes 2097152 | tf_op jit(solution)/shard_map/all_to_all | solution.py:319
  787.0 29.5 %copy-start.18 = (bf16[1,1024,4,128]{3,2,0,1:T(4,128)(2,1)}, bf16[1,1024,4,128]{3,2,0,1:T(4,128)(2,1)S(1)}, u32[]{:S(2)}) copy-start(bf16[1,1024,4,128]{3,2,0,1:T(4,128)(2,1)S(1)} %all-to-all-done.5) | copy-start | bytes 3145732
  787.0 29.5 %all-to-all-start.3 = ((bf16[1,1024,4,128]{3,2,0,1:T(4,128)(2,1)}), bf16[1,1024,4,128]{3,2,0,1:T(4,128)(2,1)}, u32[]{:S(2)}, u32[]{:S(2)}) async-start(bf16[1,1024,4,128]{3,2,0,1:T(4,128)(2,1)} %copy.143), calls=%async_computation.3 | async-start | bytes 2097152 | tf_op jit(solution)/shard_map/all_to_all | solution.py:249
  816.5 37.1 %all-to-all-start.6 = ((bf16[1,1024,4,128]{3,2,0,1:T(4,128)(2,1)}), bf16[1,1024,4,128]{3,2,0,1:T(4,128)(2,1)S(1)}, u32[]{:S(2)}, u32[]{:S(2)}) async-start(bf16[1,1024,4,128]{3,2,0,1:T(4,128)(2,1)} %copy.152), calls=%async_computation.7 | async-start | bytes 2097152 | tf_op jit(solution)/shard_map/all_to_all | solution.py:322
  820.1 181.8 %reduce-scatter.7.cloned.1.call-start = ((), (), s32[]{:S(2)}) async-start(), calls=%async_computation.18 | async-start | bytes 5242880 | tf_op jit(solution)/shard_map/reduce_scatter | solution.py:269
  837.3 23.6 %copy-start.19 = (bf16[1,1024,4,128]{3,2,0,1:T(4,128)(2,1)S(1)}, bf16[1,1024,4,128]{3,2,0,1:T(4,128)(2,1)}, u32[]{:S(2)}) copy-start(bf16[1,1024,4,128]{3,2,0,1:T(4,128)(2,1)} %copy-done.18) | copy-start | bytes 3145732
  853.7 56.8 %all-to-all-start.7 = ((bf16[1,1024,4,128]{3,2,0,1:T(4,128)(2,1)}), bf16[1,1024,4,128]{3,2,0,1:T(4,128)(2,1)}, u32[]{:S(2)}, u32[]{:S(2)}) async-start(bf16[1,1024,4,128]{3,2,0,1:T(4,128)(2,1)} %copy.154), calls=%async_computation.8 | async-start | bytes 2097152 | tf_op jit(solution)/shard_map/all_to_all | solution.py:325
  857.9 211.8 %all-reduce.28.cloned.1.call-start = ((), (), s32[]{:S(2)}) async-start(), calls=%async_computation.25 | async-start | bytes 131072
  911.9 3.0 copy-start.9
  911.9 3.0 copy-start.27
  923.0 4.7 copy-start.4
  923.0 4.8 copy-start.32
  923.0 4.8 copy-start.36
  923.0 4.8 copy-start.40
  927.8 14.6 copy-start.42
  927.8 14.7 copy-start.38
  941.7 4.6 copy-start.44
  942.4 3.9 copy-start.13
  942.4 3.9 copy-start.15
  949.8 488.3 %reduce-scatter.13.cloned.1.call-start = ((), (), s32[]{:S(2)}) async-start(), calls=%async_computation.22 | async-start | bytes 17301504 | tf_op jit(solution)/shard_map/reduce_scatter | solution.py:350
  959.5 914.9 %reduce-scatter.11.cloned.1.call-start = ((), (), s32[]{:S(2)}) async-start(), calls=%async_computation.21 | async-start | bytes 51904512 | tf_op jit(solution)/shard_map/reduce_scatter | solution.py:348
  981.8 20.0 %copy-start.10 = (bf16[1,256,4,4,128]{1,4,3,2,0:T(8,128)(2,1)S(1)}, bf16[1,256,4,4,128]{1,4,3,2,0:T(8,128)(2,1)}, u32[]{:S(2)}) copy-start(bf16[1,256,4,4,128]{1,4,3,2,0:T(8,128)(2,1)} %copy.145) | copy-start | bytes 3145732
  1070.5 804.4 %copy-start.50 = (f32[64]{0:T(128)}, f32[64]{0:T(128)S(1)}, u32[]{:S(2)}) copy-start(f32[64]{0:T(128)S(1)} %dynamic-slice.16) | copy-start | bytes 772
  (23 other events, 33.2 us)
Sparse Core Ops, SparseCore 0:
  63.2 80.5 all-gather.10
  145.3 79.2 all-gather.14
  226.5 52.9 all-gather.12
  282.2 77.2 all-gather.8
  362.3 172.8 all-gather.6
  537.3 101.5 reduce-scatter.8
  642.8 88.5 reduce-scatter.16
  734.9 71.2 reduce-scatter.14
  834.1 96.7 reduce-scatter.6
  949.9 119.8 all-reduce.27
  1072.6 365.3 reduce-scatter.12
  1444.9 429.4 reduce-scatter.10
